TPU v7x, 32 devices: a whole 2x2x4 slice. The times are simulated.
32 devices in a mesh: row: 4 (over y, x), col: 4 (over z), dp: 2 (over core).
Axes of the slice: x: 2, y: 2, z: 4, core: 2. Of those that a mesh axis runs over, the one named last changes fastest.
Arguments:
- tokens: bfloat16 [512, 8192], P(('row', 'dp'), 'col'), may hold values from -6 to 6
- upstream: bfloat16 [512, 8192], P(('row', 'dp'), 'col'), may hold values from -1.5 to 1.5
- w_gate: bfloat16 [8192, 14336], P('col', 'row'), may hold values from -0.0625 to 0.0625
- w_up: bfloat16 [8192, 14336], P('col', 'row'), may hold values from -0.0625 to 0.0625
- w_down: bfloat16 [14336, 8192], P('row', 'col'), may hold values from -0.046875 to 0.046875
- delta_gate: bfloat16 [4, 4, 192, 128, 128], P('col', 'row'), may hold values from -0.03125 to 0.03125
- delta_up: bfloat16 [4, 4, 192, 128, 128], P('col', 'row'), may hold values from -0.03125 to 0.03125
- delta_down: bfloat16 [4, 4, 192, 128, 128], P('row', 'col'), may hold values from -0.0234375 to 0.0234375
- pattern_gate: int32 [4, 4, 192], P('col', 'row'), may hold values from 0 to 448, as said below
- pattern_up: int32 [4, 4, 192], P('col', 'row'), may hold values from 0 to 448, as said below
- pattern_down: int32 [4, 4, 192], P('row', 'col'), may hold values from 0 to 448, as said below
Outputs:
- output: bfloat16 [512, 8192], P(('row', 'dp'), 'col')
- input_grad: bfloat16 [512, 8192], P(('row', 'dp'), 'col')
- delta_grad_gate: float32 [4, 4, 192, 128, 128], P('col', 'row', 'dp')
- delta_grad_up: float32 [4, 4, 192, 128, 128], P('col', 'row', 'dp')
- delta_grad_down: float32 [4, 4, 192, 128, 128], P('row', 'col', 'dp')
Inputs may be any that keep to these rules, and one draw needn't show every extreme that they name: `pattern_gate`: in each tile the 192 slots name distinct blocks of that tile; the value 448 marks an empty slot; live slots come first, a tile holds 48 to 192 of them, and some tile holds 192. `pattern_up`: as for pattern_gate. `pattern_down`: as for pattern_gate.
All inputs are finite; a program needn't handle non-finite values.
Results may differ from a plain program's by a relative error of at most 0.0058.
Values may be sent and summed in bfloat16 or wider, within the bound.
A program may use at most 320 MiB of HBM per device.

v0:
```python
import jax
import jax.numpy as jnp
from jax import lax
from jax.sharding import PartitionSpec as P


def fold_tile(weight, blocks, pattern):
    block_size = blocks.shape[-1]
    row_blocks = weight.shape[0] // block_size
    column_blocks = weight.shape[1] // block_size
    slot_list = pattern.reshape(-1)
    flat_blocks = blocks.reshape(slot_list.shape[0], block_size, block_size)
    numbers = jnp.arange(row_blocks * column_blocks, dtype=jnp.int32)
    one_hot = (slot_list[:, None] == numbers[None, :]).astype(jnp.bfloat16)
    placed = jnp.einsum("sk,sij->kij", one_hot, flat_blocks, preferred_element_type=jnp.float32)
    placed = placed.reshape(row_blocks, column_blocks, block_size, block_size)
    placed = placed.transpose(0, 2, 1, 3).reshape(weight.shape)
    return (weight.astype(jnp.float32) + placed).astype(jnp.bfloat16)


def tile_grads(left_rows, right_rows, slot_list, block_size):
    left_count = left_rows.shape[1] // block_size
    right_count = right_rows.shape[1] // block_size
    tile_blocks = left_count * right_count
    usable = (slot_list < tile_blocks).astype(jnp.float32)
    clipped = jnp.minimum(slot_list, tile_blocks - 1)
    left_pick = jnp.take(
        left_rows.reshape(left_rows.shape[0], left_count, block_size),
        clipped // right_count,
        axis=1,
    )
    right_pick = jnp.take(
        right_rows.reshape(right_rows.shape[0], right_count, block_size),
        clipped % right_count,
        axis=1,
    )
    result = jnp.einsum("tsi,tsj->sij", left_pick, right_pick, preferred_element_type=jnp.float32)
    return result * usable[:, None, None]


def dot_transposed(left_rows, right_rows):
    return lax.dot_general(
        left_rows, right_rows, (((1,), (1,)), ((), ())), preferred_element_type=jnp.float32
    )


def local(
    tokens,
    upstream,
    w_gate,
    w_up,
    w_down,
    delta_gate,
    delta_up,
    delta_down,
    pattern_gate,
    pattern_up,
    pattern_down,
):
    block_size = delta_gate.shape[-1]
    gate_folded = fold_tile(w_gate, delta_gate, pattern_gate)
    up_folded = fold_tile(w_up, delta_up, pattern_up)
    down_folded = fold_tile(w_down, delta_down, pattern_down)
    hidden_width = gate_folded.shape[1]
    joined = jnp.concatenate((gate_folded, up_folded), axis=1)
    token_all, upstream_all = (
        lax.all_gather(tokens, "row", axis=0, tiled=True),
        lax.all_gather(upstream, "row", axis=0, tiled=True),
    )
    row_block = token_all
    totals = lax.psum_scatter(
        jnp.dot(row_block, joined, preferred_element_type=jnp.float32),
        "col",
        scatter_dimension=0,
        tiled=True,
    )
    gate_mine = totals[:, :hidden_width]
    up_mine = totals[:, hidden_width:]
    hidden_mine = (gate_mine * jax.nn.sigmoid(gate_mine) * up_mine).astype(jnp.bfloat16)
    hidden_all = lax.all_gather(hidden_mine, "col", axis=0, tiled=True)
    row_block = hidden_all
    output = lax.psum_scatter(
        jnp.dot(row_block, down_folded, preferred_element_type=jnp.float32),
        "row",
        scatter_dimension=0,
        tiled=True,
    ).astype(jnp.bfloat16)
    row_block = upstream_all
    backward_mine = lax.psum_scatter(
        dot_transposed(row_block, down_folded), "col", scatter_dimension=0, tiled=True
    )
    sigmoid_mine = jax.nn.sigmoid(gate_mine)
    grad_gate = (
        backward_mine * up_mine * sigmoid_mine * (1.0 + gate_mine * (1.0 - sigmoid_mine))
    ).astype(jnp.bfloat16)
    grad_up = (backward_mine * gate_mine * sigmoid_mine).astype(jnp.bfloat16)
    grads_joined = lax.all_gather(
        jnp.concatenate((grad_gate, grad_up), axis=1), "col", axis=0, tiled=True
    )
    row_block = grads_joined
    input_grad = lax.psum_scatter(
        dot_transposed(row_block, joined), "row", scatter_dimension=0, tiled=True
    ).astype(jnp.bfloat16)
    grad_terms = (
        tile_grads(token_all, grads_joined[:, :hidden_width], pattern_gate.reshape(-1), block_size),
        tile_grads(token_all, grads_joined[:, hidden_width:], pattern_up.reshape(-1), block_size),
        tile_grads(hidden_all, upstream_all, pattern_down.reshape(-1), block_size),
    )
    grad_gate_mine, grad_up_mine, grad_down_mine = (
        lax.psum_scatter(grad_terms[0], "dp", scatter_dimension=0, tiled=True),
        lax.psum_scatter(grad_terms[1], "dp", scatter_dimension=0, tiled=True),
        lax.psum_scatter(grad_terms[2], "dp", scatter_dimension=0, tiled=True),
    )
    delta_grad_gate = grad_gate_mine.reshape((1, 1) + grad_gate_mine.shape)
    delta_grad_up = grad_up_mine.reshape((1, 1) + grad_up_mine.shape)
    delta_grad_down = grad_down_mine.reshape((1, 1) + grad_down_mine.shape)
    return (output, input_grad, delta_grad_gate, delta_grad_up, delta_grad_down)


def solution(mesh):
    return jax.shard_map(
        local,
        mesh=mesh,
        in_specs=(
            P(("row", "dp"), "col"),
            P(("row", "dp"), "col"),
            P("col", "row"),
            P("col", "row"),
            P("row", "col"),
            P("col", "row", None, None, None),
            P("col", "row", None, None, None),
            P("row", "col", None, None, None),
            P("col", "row", None),
            P("col", "row", None),
            P("row", "col", None),
        ),
        out_specs=(
            P(("row", "dp"), "col"),
            P(("row", "dp"), "col"),
            P("col", "row", "dp", None, None),
            P("col", "row", "dp", None, None),
            P("row", "col", "dp", None, None),
        ),
        check_vma=False,
    )
```

profile of v0, /device:TPU:1, one launch (start us, length us, event | category | flops | bytes accessed | tf_op | source)
XLA Modules:
  0.0 742.4 jit_solution(11663043650277400420)
XLA Ops:
  8.7 18.7 %fusion.29 = f32[16,28,128,128]{3,1,2,0:T(8,128)} fusion(bf16[192,128,128]{2,1,0:T(8,128)(2,1)} %bitcast.108, s32[16,28]{1,0:T(8,128)S(1)} %multiply_add_fusion.1, s32[192]{0:T(256)} %bitcast.117), kind=kOutput, calls=%fused_computation.41 | convolution fusion | flops 2818658304 | bytes 35654144 | tf_op jit(solution)/shard_map/sk,sij->kij/dot_general | solution.py:15
  27.5 19.3 %fusion.25 = f32[28,16,128,128]{3,1,2,0:T(8,128)} fusion(bf16[192,128,128]{2,1,0:T(8,128)(2,1)S(1)} %bitcast.111, s32[28,16]{1,0:T(8,128)S(1)} %multiply_add_fusion, s32[192]{0:T(256)S(1)} %bitcast.115), kind=kOutput, calls=%fused_computation.37 | convolution fusion | flops 2818658304 | bytes 35654144 | tf_op jit(solution)/shard_map/sk,sij->kij/dot_general | solution.py:15
  46.7 24.8 %convolution_bitcast_fusion = f32[256,3584]{0,1:T(8,128)} fusion(bf16[256,2048]{1,0:T(8,128)(2,1)} %all-gather.9.cloned.1.call-done, f32[448,8,16,128]{3,2,1,0:T(8,128)} %bitcast.99, bf16[3584,2048]{1,0:T(8,128)(2,1)} %param.19), kind=kOutput, calls=%fused_computation.52 | convolution fusion | flops 3780116480 | bytes 48758784 | tf_op jit(solution)/shard_map/dot_general | solution.py:42
  76.8 19.0 %fusion.27 = f32[16,28,128,128]{3,1,2,0:T(8,128)} fusion(bf16[192,128,128]{2,1,0:T(8,128)(2,1)} %bitcast.112, s32[192]{0:T(256)S(1)} %bitcast.119, s32[16,28]{1,0:T(8,128)S(1)} %multiply_add_fusion.1), kind=kOutput, calls=%fused_computation.39 | convolution fusion | flops 2818658304 | bytes 35654144 | tf_op jit(solution)/shard_map/sk,sij->kij/dot_general | solution.py:15
  95.8 34.6 %copy.145 = f32[256,8,28,128]{3,1,2,0:T(8,128)} copy(f32[256,8,28,128]{3,2,1,0:T(8,128)} %bitcast.101) | data formatting | bytes 58720256
  130.4 29.8 %copy.116 = f32[2048,3584]{0,1:T(8,128)} copy(f32[2048,3584]{1,0:T(8,128)} %bitcast.103) | data formatting | bytes 58720256 | tf_op jit(solution)/shard_map/reshape | solution.py:17
  160.2 34.7 %copy.144 = f32[256,8,28,128]{3,1,2,0:T(8,128)} copy(f32[256,8,28,128]{3,2,1,0:T(8,128)} %bitcast.102) | data formatting | bytes 58720256
  194.9 29.7 %copy.117 = f32[2048,3584]{0,1:T(8,128)} copy(f32[2048,3584]{1,0:T(8,128)} %bitcast.104) | data formatting | bytes 58720256 | tf_op jit(solution)/shard_map/reshape | solution.py:17
  224.6 20.4 %copy.85 = bf16[2048,3584]{0,1:T(8,128)(2,1)} copy(bf16[2048,3584]{1,0:T(8,128)(2,1)} %param.17) | data formatting | bytes 29360128 | tf_op args[2]
  244.9 20.4 %copy.88 = bf16[2048,3584]{0,1:T(8,128)(2,1)} copy(bf16[2048,3584]{1,0:T(8,128)(2,1)} %param.18) | data formatting | bytes 29360128 | tf_op args[3]
  265.3 39.0 %add_convert_fusion = (bf16[2048,3584]{0,1:T(8,128)(2,1)}, bf16[2048,3584]{0,1:T(8,128)(2,1)}) fusion(f32[2048,3584]{0,1:T(8,128)} %copy.117, bf16[2048,3584]{0,1:T(8,128)(2,1)} %copy.88, f32[2048,3584]{0,1:T(8,128)} %copy.116, bf16[2048,3584]{0,1:T(8,128)(2,1)} %copy.85), kind=kLoop, calls=%fused_computation.11 | loop fusion | flops 44040192 | bytes 117440512 | tf_op jit(solution)/shard_map/convert_element_type | solution.py:18
  304.4 16.0 %fusion.24 = f32[256,7168]{0,1:T(8,128)} fusion(bf16[256,2048]{1,0:T(8,128)(2,1)} %all-gather.5.cloned.1.call-done, bf16[2048,3584]{0,1:T(8,128)(2,1)} %get-tuple-element.33, bf16[2048,3584]{0,1:T(8,128)(2,1)} %get-tuple-element.34), kind=kOutput, calls=%fused_computation.36 | convolution fusion | flops 7574913024 | bytes 37748736 | tf_op jit(solution)/shard_map/dot_general | solution.py:72
  320.3 8.4 %copy.118 = f32[256,7168]{1,0:T(8,128)} copy(f32[256,7168]{0,1:T(8,128)} %fusion.24) | data formatting | bytes 14680064
  328.9 129.6 %reduce-scatter.22.cloned.1.call-done = f32[64,7168]{1,0:T(8,128)} async-done(((f32[256,7168]{1,0:T(8,128)}), f32[64,7168]{1,0:T(8,128)}) %reduce-scatter.22.cloned.1.call-update) | async-done | bytes 1835024 | tf_op jit(solution)/shard_map/reduce_scatter | solution.py:71
  462.6 40.7 %all-gather.7.cloned.1.call-done = bf16[256,3584]{1,0:T(8,128)(2,1)} async-done(((bf16[64,3584]{1,0:T(8,128)(2,1)}), bf16[256,3584]{1,0:T(8,128)(2,1)}) %all-gather.7.cloned.1.call-update) | async-done | bytes 1835024 | tf_op jit(solution)/shard_map/all_gather | solution.py:80
  503.3 22.8 %fusion.67 = f32[256,2048]{1,0:T(8,128)} fusion(bf16[256,3584]{1,0:T(8,128)(2,1)} %all-gather.7.cloned.1.call-done, f32[448,8,16,128]{3,2,1,0:T(8,128)} %bitcast.100, bf16[3584,2048]{1,0:T(8,128)(2,1)} %param.19), kind=kOutput, calls=%fused_computation.111 | convolution fusion | flops 3780116480 | bytes 47972352 | tf_op jit(solution)/shard_map/dot_general | solution.py:83
  526.1 50.2 %all-gather.11.cloned.1.call-done = bf16[256,7168]{1,0:T(8,128)(2,1)} async-done(((bf16[64,7168]{1,0:T(8,128)(2,1)}), bf16[256,7168]{1,0:T(8,128)(2,1)}) %all-gather.11.cloned.1.call-update) | async-done | bytes 3670032 | tf_op jit(solution)/shard_map/all_gather | solution.py:97
  576.4 15.2 %fusion.1 = f32[256,2048]{1,0:T(8,128)} fusion(bf16[256,7168]{1,0:T(8,128)(2,1)} %all-gather.11.cloned.1.call-done, bf16[2048,3584]{0,1:T(8,128)(2,1)} %get-tuple-element.33, bf16[2048,3584]{0,1:T(8,128)(2,1)} %get-tuple-element.34), kind=kOutput, calls=%fused_computation.13 | convolution fusion | flops 7574913024 | bytes 35127296 | tf_op jit(solution)/shard_map/dot_general | solution.py:42
  606.7 8.3 %gather_fusion.4 = bf16[192,256,128]{2,1,0:T(8,128)(2,1)} fusion(bf16[256,28,128]{2,0,1:T(8,128)(2,1)S(1)} %copy.106, s32[1024]{0:T(1024)S(1)} %get-tuple-element.40), kind=kCustom, calls=%fused_computation.5.clone | custom fusion | bytes 25166592 | tf_op jit(solution)/shard_map/jit(_take)/gather | solution.py:27
  615.0 13.9 %broadcast_multiply_fusion = f32[192,128,128]{2,1,0:T(8,128)} fusion(f32[192]{0:T(256)S(1)} %get-tuple-element.26, bf16[192,256,128]{2,1,0:T(8,128)(2,1)} %gather_fusion.5, pred[192]{0:T(512)(128)(4,1)S(1)} %get-tuple-element.24, bf16[192,256,128]{2,1,0:T(8,128)(2,1)} %gather_fusion.4, pred[192]{0:T(512)(128)(4,1)S(1)} %get-tuple-element.7), kind=kOutput, calls=%fused_computation.49 | convolution fusion | flops 1626341376 | bytes 37749888 | tf_op jit(solution)/shard_map/tsi,tsj->sij/dot_general | solution.py:37
  656.0 18.6 %broadcast_multiply_fusion.2 = f32[192,128,128]{2,1,0:T(8,128)} fusion(f32[192]{0:T(256)S(1)} %get-tuple-element.32, bf16[192,256,128]{2,1,0:T(8,128)(2,1)} %gather_fusion.1, pred[192]{0:T(512)(128)(4,1)S(1)} %get-tuple-element.30, bf16[192,256,128]{2,1,0:T(8,128)(2,1)} %gather_fusion, pred[192]{0:T(512)(128)(4,1)S(1)} %get-tuple-element.15), kind=kOutput, calls=%fused_computation.51 | convolution fusion | flops 1626341376 | bytes 37749888 | tf_op jit(solution)/shard_map/tsi,tsj->sij/dot_general | solution.py:37
  688.7 10.4 %gather_fusion.3 = bf16[192,256,128]{2,1,0:T(8,128)(2,1)} fusion(bf16[256,28,128]{2,0,1:T(8,128)(2,1)S(1)} %copy.103, s32[1024]{0:T(1024)S(1)} %get-tuple-element.37), kind=kCustom, calls=%fused_computation.4.clone | custom fusion | bytes 25166592 | tf_op jit(solution)/shard_map/jit(_take)/gather | solution.py:32
  699.1 14.6 %broadcast_multiply_fusion.1 = f32[192,128,128]{2,1,0:T(8,128)} fusion(f32[192]{0:T(256)S(1)} %get-tuple-element.29, bf16[192,256,128]{2,1,0:T(8,128)(2,1)} %gather_fusion.3, pred[192]{0:T(512)(128)(4,1)S(1)} %get-tuple-element.27, bf16[192,256,128]{2,1,0:T(8,128)(2,1)} %gather_fusion.2, pred[192]{0:T(512)(128)(4,1)S(1)} %get-tuple-element.11), kind=kOutput, calls=%fused_computation.50 | convolution fusion | flops 1626341376 | bytes 37749888 | tf_op jit(solution)/shard_map/tsi,tsj->sij/dot_general | solution.py:37
  717.3 18.3 %reduce-scatter.18.cloned.1.call-done = f32[96,128,128]{2,1,0:T(8,128)} async-done(((f32[192,128,128]{2,1,0:T(8,128)}), f32[96,128,128]{2,1,0:T(8,128)}) %reduce-scatter.18.cloned.1.call-update) | async-done | bytes 6291472 | tf_op jit(solution)/shard_map/reduce_scatter | solution.py:111
  (80 shorter events, 70.8 us)
Async XLA Ops:
  7.2 39.6 %all-gather.9.cloned.1.call-start = ((), (), s32[]{:S(2)}) async-start(), calls=%async_computation.10 | async-start | bytes 1310720 | tf_op jit(solution)/shard_map/all_gather | solution.py:68
  7.2 20.2 %slice-start = ((s8[6291456]{0:T(1024)(128)(4,1)}), s8[2097152]{0:T(1024)(128)(4,1)S(1)}, s32[]{:S(2)}) async-start(s8[6291456]{0:T(1024)(128)(4,1)} %bitcast.109), calls=%async_computation.18 | async-start | bytes 4194304
  7.9 296.5 %all-gather.5.cloned.1.call-start = ((), (), s32[]{:S(2)}) async-start(), calls=%async_computation.7 | async-start | bytes 1310720 | tf_op jit(solution)/shard_map/all_gather | solution.py:67
  8.6 320.2 %reduce-scatter.24.cloned.1.call-start = ((), (), s32[]{:S(2)}) async-start(), calls=%async_computation.17 | async-start | bytes 4587520 | tf_op jit(solution)/shard_map/reduce_scatter | solution.py:89
  8.7 18.7 %slice-start.1 = ((s8[6291456]{0:T(1024)(128)(4,1)}), s8[4194304]{0:T(1024)(128)(4,1)S(1)}, s32[]{:S(2)}) async-start(s8[6291456]{0:T(1024)(128)(4,1)} %bitcast.109), calls=%async_computation.19 | async-start | bytes 8388608
  8.7 18.7 %copy-start.4 = (s32[1,1,192]{2,1,0:T(1,128)S(1)}, s32[1,1,192]{2,1,0:T(1,128)}, u32[]{:S(2)}) copy-start(s32[1,1,192]{2,1,0:T(1,128)} %param.25) | copy-start | bytes 2308
  46.7 30.0 %copy-start.7 = (s32[1,1,192]{2,1,0:T(1,128)S(1)}, s32[1,1,192]{2,1,0:T(1,128)}, u32[]{:S(2)}) copy-start(s32[1,1,192]{2,1,0:T(1,128)} %param.24) | copy-start | bytes 2308
  76.7 381.8 %reduce-scatter.22.cloned.1.call-start = ((), (), s32[]{:S(2)}) async-start(), calls=%async_computation.16 | async-start | bytes 9175040 | tf_op jit(solution)/shard_map/reduce_scatter | solution.py:71
  328.8 174.5 %all-gather.7.cloned.1.call-start = ((), (), s32[]{:S(2)}) async-start(), calls=%async_computation.8 | async-start | bytes 2293760 | tf_op jit(solution)/shard_map/all_gather | solution.py:80
  461.5 114.9 %all-gather.11.cloned.1.call-start = ((), (), s32[]{:S(2)}) async-start(), calls=%async_computation.11 | async-start | bytes 4587520 | tf_op jit(solution)/shard_map/all_gather | solution.py:97
  462.6 251.2 %reduce-scatter.12.cloned.1.call-start = ((), (), s32[]{:S(2)}) async-start(), calls=%async_computation.9 | async-start | bytes 2621440 | tf_op jit(solution)/shard_map/reduce_scatter | solution.py:82
  526.1 65.6 %copy-start.5 = (s32[1,1,192]{2,1,0:T(1,128)S(1)}, s32[1,1,192]{2,1,0:T(1,128)}, u32[]{:S(2)}) copy-start(s32[1,1,192]{2,1,0:T(1,128)} %param.25) | copy-start | bytes 2308
  526.1 65.6 %copy-start.2 = (bf16[256,2048]{1,0:T(8,128)(2,1)S(1)}, bf16[256,2048]{1,0:T(8,128)(2,1)}, u32[]{:S(2)}) copy-start(bf16[256,2048]{1,0:T(8,128)(2,1)} %all-gather.9.cloned.1.call-done) | copy-start | bytes 3145732
  526.1 189.5 %reduce-scatter.14.cloned.1.call-start = ((), (), s32[]{:S(2)}) async-start(), calls=%async_computation.12 | async-start | bytes 2621440 | tf_op jit(solution)/shard_map/reduce_scatter | solution.py:101
  591.6 125.7 %reduce-scatter.20.cloned.1.call-start = ((), (), s32[]{:S(2)}) async-start(), calls=%async_computation.15 | async-start | bytes 18874368 | tf_op jit(solution)/shard_map/reduce_scatter | solution.py:112
  593.3 8.2 %copy-start.1 = (bf16[256,3584]{1,0:T(8,128)(2,1)S(1)}, bf16[256,3584]{1,0:T(8,128)(2,1)}, u32[]{:S(2)}) copy-start(bf16[256,3584]{1,0:T(8,128)(2,1)} %all-gather.7.cloned.1.call-done) | copy-start | bytes 5505028
  628.9 0.7 copy-start.6
  628.9 1.2 copy-start.3
  628.9 88.4 %reduce-scatter.16.cloned.1.call-start = ((), (), s32[]{:S(2)}) async-start(), calls=%async_computation.13 | async-start | bytes 18874368 | tf_op jit(solution)/shard_map/reduce_scatter | solution.py:110
  674.6 0.7 copy-start.8
  674.6 61.0 %reduce-scatter.18.cloned.1.call-start = ((), (), s32[]{:S(2)}) async-start(), calls=%async_computation.14 | async-start | bytes 18874368 | tf_op jit(solution)/shard_map/reduce_scatter | solution.py:111
  675.3 8.1 %copy-start = (bf16[256,3584]{1,0:T(8,128)(2,1)S(1)}, bf16[256,3584]{1,0:T(8,128)(2,1)}, u32[]{:S(2)}) copy-start(bf16[256,3584]{1,0:T(8,128)(2,1)} %get-tuple-element.19) | copy-start | bytes 5505028
Sparse Core Ops, SparseCore 0:
  9.8 28.3 all-gather.8
  40.1 26.4 all-gather.4
  76.8 70.0 reduce-scatter.23
  328.9 129.5 reduce-scatter.21
  461.6 41.6 all-gather.6
  505.3 71.0 all-gather.10
  579.3 33.7 reduce-scatter.11
  616.0 35.1 reduce-scatter.13
  654.2 22.4 reduce-scatter.19
  679.4 23.1 reduce-scatter.15
  713.9 21.7 reduce-scatter.17
where the time goes:
time: 753 us; the launch traced here: 742 us
  local copies, waits for them, and re-layouts  258 us (34%)
  waiting for transfers between devices  240 us (32%)
  matrix products  183 us (24%)
  other arithmetic  46.7 us (6%)
  between operations  14.3 us (2%)
    unnamed x30, local copies, waits for them, and re-layouts  130 us
    reduce_scatter x1, waiting for transfers between devices, local(): lax.psum_scatter(jnp.dot(row_block, joined, preferred_element_type=jnp.fl...  130 us
    reshape x2, local copies, waits for them, and re-layouts, fold_tile(): placed = placed.transpose(0, 2, 1, 3).reshape(weight.shape)  59.5 us
    dot_general x3, matrix products, fold_tile(): jnp.einsum('sk,sij->kij', one_hot, flat_blocks, preferred_element_type=jn...  57 us
    all_gather x1, waiting for transfers between devices, local(): lax.all_gather(jnp.concatenate((grad_gate, grad_up), axis=1), 'col', axis...  50.2 us
    dot_general x3, matrix products, tile_grads(): jnp.einsum('tsi,tsj->sij', left_pick, right_pick, preferred_element_type=...  47 us
    all_gather x1, waiting for transfers between devices, local(): hidden_all = lax.all_gather(hidden_mine, 'col', axis=0, tiled=True)  40.7 us
    dot_general x2, matrix products, dot_transposed(): lax.dot_general(left_rows, right_rows, (((1,), (1,)), ((), ())), preferre...  40 us
  transfers between devices with their start and end apart: 11, of which 4 were waited for; matrix products, arithmetic and copies ran while one was open for 65% of the time, Pallas kernels for 0%

commit v1 on v0

--- a/solution.py
+++ b/solution.py
@@ -77,7 +77,12 @@
     gate_mine = totals[:, :hidden_width]
     up_mine = totals[:, hidden_width:]
     hidden_mine = (gate_mine * jax.nn.sigmoid(gate_mine) * up_mine).astype(jnp.bfloat16)
-    hidden_all = lax.all_gather(hidden_mine, "col", axis=0, tiled=True)
+    ring = [hidden_mine]
+    for hop in range(3):
+        ring.append(lax.ppermute(ring[-1], "col", [(dev, (dev + 1) % 4) for dev in range(4)]))
+    hidden_all = jnp.roll(
+        jnp.concatenate(ring[::-1], axis=0), (lax.axis_index("col") + 1) * ring[0].shape[0], axis=0
+    )
     row_block = hidden_all
     output = lax.psum_scatter(
         jnp.dot(row_block, down_folded, preferred_element_type=jnp.float32),

time: 753 us -> 742 us (0.985)
  waiting for transfers between devices: 240 us -> 226 us
    all_gather x1 -> x0, waiting for transfers between devices: 40.7 us -> none  [local(): hidden_all = lax.all_gather(hidden_mine, 'col', axis=0, tiled=True)]
    ppermute x0 -> x3, waiting for transfers between devices: none -> 34.6 us  [local(): lax.ppermute(ring[-1], 'col', [(dev, (dev + 1) % 4) for dev in range(4)])]
    all_gather x1, waiting for transfers between devices: 50.2 us -> 42.3 us  [local(): lax.all_gather(jnp.concatenate((grad_gate, grad_up), axis=1), 'col', axis...]
    unnamed x30 -> x35, local copies, waits for them, and re-layouts: 130 us -> 130 us
  transfers between devices with their start and end apart: 11 -> 13, of which waited for: 4 -> 6; matrix products, arithmetic and copies ran while one was open for 65% -> 66% of each run, Pallas kernels for 0% -> 0%
where the time goes in v1:
time: 742 us; the launch traced here: 731 us
  local copies, waits for them, and re-layouts  259 us (35%)
  waiting for transfers between devices  226 us (30%)
  matrix products  184 us (25%)
  other arithmetic  45.9 us (6%)
  between operations  14.7 us (2%)
    unnamed x35, local copies, waits for them, and re-layouts  130 us
    reduce_scatter x1, waiting for transfers between devices, local(): lax.psum_scatter(jnp.dot(row_block, joined, preferred_element_type=jnp.fl...  130 us
    reshape x2, local copies, waits for them, and re-layouts, fold_tile(): placed = placed.transpose(0, 2, 1, 3).reshape(weight.shape)  59.4 us
    dot_general x3, matrix products, fold_tile(): jnp.einsum('sk,sij->kij', one_hot, flat_blocks, preferred_element_type=jn...  57 us
    dot_general x3, matrix products, tile_grads(): jnp.einsum('tsi,tsj->sij', left_pick, right_pick, preferred_element_type=...  48.6 us
    all_gather x1, waiting for transfers between devices, local(): lax.all_gather(jnp.concatenate((grad_gate, grad_up), axis=1), 'col', axis...  42.3 us
    dot_general x2, matrix products, dot_transposed(): lax.dot_general(left_rows, right_rows, (((1,), (1,)), ((), ())), preferre...  40.1 us
    convert_element_type x1, other arithmetic, fold_tile(): return (weight.astype(jnp.float32) + placed).astype(jnp.bfloat16)  39 us
  transfers between devices with their start and end apart: 13, of which 6 were waited for; matrix products, arithmetic and copies ran while one was open for 66% of the time, Pallas kernels for 0%

profile of v1, /device:TPU:1, one launch (start us, length us, event | category | flops | bytes accessed | tf_op | source)
XLA Modules:
  0.0 730.8 jit_solution(706147929298305518)
XLA Ops:
  8.7 18.7 %fusion.29 = f32[16,28,128,128]{3,1,2,0:T(8,128)} fusion(bf16[192,128,128]{2,1,0:T(8,128)(2,1)} %bitcast.108, s32[16,28]{1,0:T(8,128)S(1)} %multiply_add_fusion.1, s32[192]{0:T(256)} %bitcast.117), kind=kOutput, calls=%fused_computation.41 | convolution fusion | flops 2818658304 | bytes 35654144 | tf_op jit(solution)/shard_map/sk,sij->kij/dot_general | solution.py:15
  27.5 19.3 %fusion.25 = f32[28,16,128,128]{3,1,2,0:T(8,128)} fusion(bf16[192,128,128]{2,1,0:T(8,128)(2,1)S(1)} %bitcast.111, s32[28,16]{1,0:T(8,128)S(1)} %multiply_add_fusion, s32[192]{0:T(256)S(1)} %bitcast.115), kind=kOutput, calls=%fused_computation.37 | convolution fusion | flops 2818658304 | bytes 35654144 | tf_op jit(solution)/shard_map/sk,sij->kij/dot_general | solution.py:15
  46.7 24.8 %convolution_bitcast_fusion = f32[256,3584]{0,1:T(8,128)} fusion(bf16[256,2048]{1,0:T(8,128)(2,1)} %all-gather.6.cloned.1.call-done, f32[448,8,16,128]{3,2,1,0:T(8,128)} %bitcast.99, bf16[3584,2048]{1,0:T(8,128)(2,1)} %param.19), kind=kOutput, calls=%fused_computation.52 | convolution fusion | flops 3780116480 | bytes 48758784 | tf_op jit(solution)/shard_map/dot_general | solution.py:42
  76.8 19.0 %fusion.27 = f32[16,28,128,128]{3,1,2,0:T(8,128)} fusion(bf16[192,128,128]{2,1,0:T(8,128)(2,1)} %bitcast.112, s32[192]{0:T(256)S(1)} %bitcast.119, s32[16,28]{1,0:T(8,128)S(1)} %multiply_add_fusion.1), kind=kOutput, calls=%fused_computation.39 | convolution fusion | flops 2818658304 | bytes 35654144 | tf_op jit(solution)/shard_map/sk,sij->kij/dot_general | solution.py:15
  95.8 34.6 %copy.176 = f32[256,8,28,128]{3,1,2,0:T(8,128)} copy(f32[256,8,28,128]{3,2,1,0:T(8,128)} %bitcast.101) | data formatting | bytes 58720256
  130.4 29.7 %copy.147 = f32[2048,3584]{0,1:T(8,128)} copy(f32[2048,3584]{1,0:T(8,128)} %bitcast.103) | data formatting | bytes 58720256 | tf_op jit(solution)/shard_map/reshape | solution.py:17
  160.1 34.7 %copy.175 = f32[256,8,28,128]{3,1,2,0:T(8,128)} copy(f32[256,8,28,128]{3,2,1,0:T(8,128)} %bitcast.102) | data formatting | bytes 58720256
  194.9 29.7 %copy.148 = f32[2048,3584]{0,1:T(8,128)} copy(f32[2048,3584]{1,0:T(8,128)} %bitcast.104) | data formatting | bytes 58720256 | tf_op jit(solution)/shard_map/reshape | solution.py:17
  224.6 20.4 %copy.116 = bf16[2048,3584]{0,1:T(8,128)(2,1)} copy(bf16[2048,3584]{1,0:T(8,128)(2,1)} %param.17) | data formatting | bytes 29360128 | tf_op args[2]
  245.0 20.4 %copy.119 = bf16[2048,3584]{0,1:T(8,128)(2,1)} copy(bf16[2048,3584]{1,0:T(8,128)(2,1)} %param.18) | data formatting | bytes 29360128 | tf_op args[3]
  265.3 39.0 %add_convert_fusion = (bf16[2048,3584]{0,1:T(8,128)(2,1)}, bf16[2048,3584]{0,1:T(8,128)(2,1)}) fusion(f32[2048,3584]{0,1:T(8,128)} %copy.148, bf16[2048,3584]{0,1:T(8,128)(2,1)} %copy.119, f32[2048,3584]{0,1:T(8,128)} %copy.147, bf16[2048,3584]{0,1:T(8,128)(2,1)} %copy.116), kind=kLoop, calls=%fused_computation.11 | loop fusion | flops 44040192 | bytes 117440512 | tf_op jit(solution)/shard_map/convert_element_type | solution.py:18
  304.4 15.9 %fusion.24 = f32[256,7168]{0,1:T(8,128)} fusion(bf16[256,2048]{1,0:T(8,128)(2,1)} %all-gather.4.cloned.1.call-done, bf16[2048,3584]{0,1:T(8,128)(2,1)} %get-tuple-element.33, bf16[2048,3584]{0,1:T(8,128)(2,1)} %get-tuple-element.34), kind=kOutput, calls=%fused_computation.36 | convolution fusion | flops 7574913024 | bytes 37748736 | tf_op jit(solution)/shard_map/dot_general | solution.py:72
  328.8 129.6 %reduce-scatter.22.cloned.1.call-done = f32[64,7168]{1,0:T(8,128)} async-done(((f32[256,7168]{1,0:T(8,128)}), f32[64,7168]{1,0:T(8,128)}) %reduce-scatter.22.cloned.1.call-update) | async-done | bytes 1835024 | tf_op jit(solution)/shard_map/reduce_scatter | solution.py:71
  461.9 12.0 %collective-permute-done = bf16[64,3584]{1,0:T(8,128)(2,1)S(1)} collective-permute-done((bf16[64,3584]{1,0:T(8,128)(2,1)S(1)}, bf16[64,3584]{1,0:T(8,128)(2,1)S(1)}, u32[]{:S(2)}, u32[]{:S(2)}) %collective-permute-start) | collective-permute-done | bytes 458784 | tf_op jit(solution)/shard_map/ppermute | solution.py:82
  473.8 12.3 %collective-permute-done.1 = bf16[64,3584]{1,0:T(8,128)(2,1)S(1)} collective-permute-done((bf16[64,3584]{1,0:T(8,128)(2,1)S(1)}, bf16[64,3584]{1,0:T(8,128)(2,1)S(1)}, u32[]{:S(2)}, u32[]{:S(2)}) %collective-permute-start.1) | collective-permute-done | bytes 458784 | tf_op jit(solution)/shard_map/ppermute | solution.py:82
  487.2 10.4 %collective-permute-done.2 = bf16[64,3584]{1,0:T(8,128)(2,1)S(1)} collective-permute-done((bf16[64,3584]{1,0:T(8,128)(2,1)S(1)}, bf16[64,3584]{1,0:T(8,128)(2,1)S(1)}, u32[]{:S(2)}, u32[]{:S(2)}) %collective-permute-start.2) | collective-permute-done | bytes 458784 | tf_op jit(solution)/shard_map/ppermute | solution.py:82
  498.0 22.0 %fusion.67 = f32[256,2048]{1,0:T(8,128)} fusion(bf16[256,3584]{1,0:T(8,128)(2,1)S(1)} %constant_dynamic-slice_fusion, f32[448,8,16,128]{3,2,1,0:T(8,128)} %bitcast.100, bf16[3584,2048]{1,0:T(8,128)(2,1)} %param.19), kind=kOutput, calls=%fused_computation.120 | convolution fusion | flops 3780116480 | bytes 47972352 | tf_op jit(solution)/shard_map/dot_general | solution.py:88
  520.1 42.3 %all-gather.8.cloned.1.call-done = bf16[256,7168]{1,0:T(8,128)(2,1)} async-done(((bf16[64,7168]{1,0:T(8,128)(2,1)}), bf16[256,7168]{1,0:T(8,128)(2,1)}) %all-gather.8.cloned.1.call-update) | async-done | bytes 3670032 | tf_op jit(solution)/shard_map/all_gather | solution.py:102
  562.4 15.3 %fusion.1 = f32[256,2048]{1,0:T(8,128)} fusion(bf16[256,7168]{1,0:T(8,128)(2,1)} %all-gather.8.cloned.1.call-done, bf16[2048,3584]{0,1:T(8,128)(2,1)} %get-tuple-element.33, bf16[2048,3584]{0,1:T(8,128)(2,1)} %get-tuple-element.34), kind=kOutput, calls=%fused_computation.13 | convolution fusion | flops 7574913024 | bytes 35127296 | tf_op jit(solution)/shard_map/dot_general | solution.py:42
  602.8 14.2 %broadcast_multiply_fusion = f32[192,128,128]{2,1,0:T(8,128)} fusion(f32[192]{0:T(256)S(1)} %get-tuple-element.26, bf16[192,256,128]{2,1,0:T(8,128)(2,1)} %gather_fusion.5, pred[192]{0:T(512)(128)(4,1)S(1)} %get-tuple-element.24, bf16[192,256,128]{2,1,0:T(8,128)(2,1)} %gather_fusion.4, pred[192]{0:T(512)(128)(4,1)S(1)} %get-tuple-element.7), kind=kOutput, calls=%fused_computation.49 | convolution fusion | flops 1626341376 | bytes 37749888 | tf_op jit(solution)/shard_map/tsi,tsj->sij/dot_general | solution.py:37
  644.6 20.4 %broadcast_multiply_fusion.2 = f32[192,128,128]{2,1,0:T(8,128)} fusion(f32[192]{0:T(256)S(1)} %get-tuple-element.32, bf16[192,256,128]{2,1,0:T(8,128)(2,1)} %gather_fusion.1, pred[192]{0:T(512)(128)(4,1)S(1)} %get-tuple-element.30, bf16[192,256,128]{2,1,0:T(8,128)(2,1)} %gather_fusion, pred[192]{0:T(512)(128)(4,1)S(1)} %get-tuple-element.15), kind=kOutput, calls=%fused_computation.51 | convolution fusion | flops 1626341376 | bytes 37749888 | tf_op jit(solution)/shard_map/tsi,tsj->sij/dot_general | solution.py:37
  679.7 8.8 %gather_fusion.3 = bf16[192,256,128]{2,1,0:T(8,128)(2,1)} fusion(bf16[256,28,128]{2,0,1:T(8,128)(2,1)S(1)} %copy.134, s32[1024]{0:T(1024)S(1)} %get-tuple-element.39), kind=kCustom, calls=%fused_computation.4.clone | custom fusion | bytes 25166592 | tf_op jit(solution)/shard_map/jit(_take)/gather | solution.py:32
  688.5 14.0 %broadcast_multiply_fusion.1 = f32[192,128,128]{2,1,0:T(8,128)} fusion(f32[192]{0:T(256)S(1)} %get-tuple-element.29, bf16[192,256,128]{2,1,0:T(8,128)(2,1)} %gather_fusion.3, pred[192]{0:T(512)(128)(4,1)S(1)} %get-tuple-element.27, bf16[192,256,128]{2,1,0:T(8,128)(2,1)} %gather_fusion.2, pred[192]{0:T(512)(128)(4,1)S(1)} %get-tuple-element.11), kind=kOutput, calls=%fused_computation.50 | convolution fusion | flops 1626341376 | bytes 37749888 | tf_op jit(solution)/shard_map/tsi,tsj->sij/dot_general | solution.py:37
  706.1 17.6 %reduce-scatter.18.cloned.1.call-done = f32[96,128,128]{2,1,0:T(8,128)} async-done(((f32[192,128,128]{2,1,0:T(8,128)}), f32[96,128,128]{2,1,0:T(8,128)}) %reduce-scatter.18.cloned.1.call-update) | async-done | bytes 6291472 | tf_op jit(solution)/shard_map/reduce_scatter | solution.py:116
  (90 shorter events, 91.0 us)
Async XLA Ops:
  7.2 39.6 %all-gather.6.cloned.1.call-start = ((), (), s32[]{:S(2)}) async-start(), calls=%async_computation.9 | async-start | bytes 1310720 | tf_op jit(solution)/shard_map/all_gather | solution.py:68
  7.2 20.2 %slice-start = ((s8[6291456]{0:T(1024)(128)(4,1)}), s8[2097152]{0:T(1024)(128)(4,1)S(1)}, s32[]{:S(2)}) async-start(s8[6291456]{0:T(1024)(128)(4,1)} %bitcast.109), calls=%async_computation.17 | async-start | bytes 4194304
  7.9 296.5 %all-gather.4.cloned.1.call-start = ((), (), s32[]{:S(2)}) async-start(), calls=%async_computation.7 | async-start | bytes 1310720 | tf_op jit(solution)/shard_map/all_gather | solution.py:67
  8.6 320.1 %reduce-scatter.24.cloned.1.call-start = ((), (), s32[]{:S(2)}) async-start(), calls=%async_computation.16 | async-start | bytes 4587520 | tf_op jit(solution)/shard_map/reduce_scatter | solution.py:94
  8.7 18.7 %slice-start.1 = ((s8[6291456]{0:T(1024)(128)(4,1)}), s8[4194304]{0:T(1024)(128)(4,1)S(1)}, s32[]{:S(2)}) async-start(s8[6291456]{0:T(1024)(128)(4,1)} %bitcast.109), calls=%async_computation.18 | async-start | bytes 8388608
  8.7 18.7 %copy-start.3 = (s32[1,1,192]{2,1,0:T(1,128)S(1)}, s32[1,1,192]{2,1,0:T(1,128)}, u32[]{:S(2)}) copy-start(s32[1,1,192]{2,1,0:T(1,128)} %param.25) | copy-start | bytes 2308
  46.7 30.0 %copy-start.6 = (s32[1,1,192]{2,1,0:T(1,128)S(1)}, s32[1,1,192]{2,1,0:T(1,128)}, u32[]{:S(2)}) copy-start(s32[1,1,192]{2,1,0:T(1,128)} %param.24) | copy-start | bytes 2308
  76.7 381.7 %reduce-scatter.22.cloned.1.call-start = ((), (), s32[]{:S(2)}) async-start(), calls=%async_computation.15 | async-start | bytes 9175040 | tf_op jit(solution)/shard_map/reduce_scatter | solution.py:71
  328.7 233.6 %all-gather.8.cloned.1.call-start = ((), (), s32[]{:S(2)}) async-start(), calls=%async_computation.10 | async-start | bytes 4587520 | tf_op jit(solution)/shard_map/all_gather | solution.py:102
  460.7 13.2 %collective-permute-start = (bf16[64,3584]{1,0:T(8,128)(2,1)S(1)}, bf16[64,3584]{1,0:T(8,128)(2,1)S(1)}, u32[]{:S(2)}, u32[]{:S(2)}) collective-permute-start(bf16[64,3584]{1,0:T(8,128)(2,1)S(1)} %get-tuple-element.23), channel_id=1, source_target_pairs={{0,2},{2,4},{4,6},{6,0},{1,3},{3,5},{5,7},{7,1},{8,10},{10,12},{12... | collective-permute-start | bytes 1376264 | tf_op jit(solution)/shard_map/ppermute | solution.py:82
  473.8 12.3 %collective-permute-start.1 = (bf16[64,3584]{1,0:T(8,128)(2,1)S(1)}, bf16[64,3584]{1,0:T(8,128)(2,1)S(1)}, u32[]{:S(2)}, u32[]{:S(2)}) collective-permute-start(bf16[64,3584]{1,0:T(8,128)(2,1)S(1)} %collective-permute-done), channel_id=1, source_target_pairs={{0,2},{2,4},{4,6},{6,0},{1,3},{3,5},{5,7},{7,1},{8,10},{10,12},{12... | collective-permute-start | bytes 1376264 | tf_op jit(solution)/shard_map/ppermute | solution.py:82
  486.1 11.4 %collective-permute-start.2 = (bf16[64,3584]{1,0:T(8,128)(2,1)S(1)}, bf16[64,3584]{1,0:T(8,128)(2,1)S(1)}, u32[]{:S(2)}, u32[]{:S(2)}) collective-permute-start(bf16[64,3584]{1,0:T(8,128)(2,1)S(1)} %collective-permute-done.1), channel_id=1, source_target_pairs={{0,2},{2,4},{4,6},{6,0},{1,3},{3,5},{5,7},{7,1},{8,10},{10,12},{12... | collective-permute-start | bytes 1376264 | tf_op jit(solution)/shard_map/ppermute | solution.py:82
  487.1 215.4 %reduce-scatter.12.cloned.1.call-start = ((), (), s32[]{:S(2)}) async-start(), calls=%async_computation.8 | async-start | bytes 2621440 | tf_op jit(solution)/shard_map/reduce_scatter | solution.py:87
  520.0 57.7 %copy-start.4 = (s32[1,1,192]{2,1,0:T(1,128)S(1)}, s32[1,1,192]{2,1,0:T(1,128)}, u32[]{:S(2)}) copy-start(s32[1,1,192]{2,1,0:T(1,128)} %param.25) | copy-start | bytes 2308
  520.0 57.7 %copy-start.1 = (bf16[256,2048]{1,0:T(8,128)(2,1)S(1)}, bf16[256,2048]{1,0:T(8,128)(2,1)}, u32[]{:S(2)}) copy-start(bf16[256,2048]{1,0:T(8,128)(2,1)} %all-gather.6.cloned.1.call-done) | copy-start | bytes 3145732
  520.0 184.2 %reduce-scatter.14.cloned.1.call-start = ((), (), s32[]{:S(2)}) async-start(), calls=%async_computation.11 | async-start | bytes 2621440 | tf_op jit(solution)/shard_map/reduce_scatter | solution.py:106
  577.7 128.4 %reduce-scatter.20.cloned.1.call-start = ((), (), s32[]{:S(2)}) async-start(), calls=%async_computation.14 | async-start | bytes 18874368 | tf_op jit(solution)/shard_map/reduce_scatter | solution.py:117
  617.0 0.7 copy-start.5
  617.0 1.3 copy-start.2
  617.1 89.0 %reduce-scatter.16.cloned.1.call-start = ((), (), s32[]{:S(2)}) async-start(), calls=%async_computation.12 | async-start | bytes 18874368 | tf_op jit(solution)/shard_map/reduce_scatter | solution.py:115
  665.0 0.7 copy-start.7
  665.0 58.7 %reduce-scatter.18.cloned.1.call-start = ((), (), s32[]{:S(2)}) async-start(), calls=%async_computation.13 | async-start | bytes 18874368 | tf_op jit(solution)/shard_map/reduce_scatter | solution.py:116
  665.7 8.5 %copy-start = (bf16[256,3584]{1,0:T(8,128)(2,1)S(1)}, bf16[256,3584]{1,0:T(8,128)(2,1)}, u32[]{:S(2)}) copy-start(bf16[256,3584]{1,0:T(8,128)(2,1)} %get-tuple-element.19) | copy-start | bytes 5505028
Sparse Core Ops, SparseCore 0:
  9.8 28.3 all-gather.5
  40.1 26.4 all-gather.3
  76.8 70.0 reduce-scatter.23
  328.8 129.5 reduce-scatter.21
  487.3 75.0 all-gather.7
  565.2 33.7 reduce-scatter.11
  601.9 35.1 reduce-scatter.13
  640.0 22.6 reduce-scatter.19
  665.6 22.9 reduce-scatter.15
  702.6 21.0 reduce-scatter.17
